TPU v7x, 32 devices: a whole 2x2x4 slice. The times are simulated.
32 devices in a mesh: date: 2 (over y), trade: 8 (over z, x), path: 2 (over core).
Axes of the slice: x: 2, y: 2, z: 4, core: 2. Of those that a mesh axis runs over, the one named last changes fastest.
Arguments:
- basis_values: bfloat16 [2048, 512], P(('date', 'path')), parts along dimension 0, may hold values from -6 to 6
- coefficients: bfloat16 [2560, 512], P(('date', 'trade')), parts along dimension 0, may hold values from -0.25 to 0.25
- trade_cpty: int32 [1280], P('trade'), may hold values from 0 to 127, as said below
- trade_bucket: int32 [1280], P('trade'), may hold values from 0 to 127
- risk_weights: float32 [128], replicated, may hold values from 0.5 to 2
- correlation: float32 [128, 128], replicated, may hold values from 0 to 1, as said below
- funding_spread: float32 [128], P('trade'), may hold values from 0.5 to 2
Outputs:
- margin: float32 [128, 2048], P('trade', ('date', 'path')), parts along dimension 1
- basis_adjoint: bfloat16 [2048, 512], P(('date', 'path')), parts along dimension 0
There are 2 independent parts, one for each index of `date`. A program takes and returns all parts, laid end to end along the dimension named above; an argument that names none is the same for every part. Nothing has to cross between parts.
Inputs may be any that keep to these rules, and one draw needn't show every extreme that they name: `trade_cpty`: counterparty c belongs to owner block c // 16. Among the trades of one device, at most 40 belong to counterparties of one owner block; in every draw one owner block receives exactly 40 from every device. Counterparties differ in size. `correlation`: symmetric positive definite with unit diagonal; smallest eigenvalue at least 0.01; entries positive.
All inputs are finite; a program needn't handle non-finite values.
Results may differ from a plain program's by a relative error of at most 0.0034.
Values may be sent and summed in bfloat16 or wider, within the bound.
No kernel may reach another device: no remote copies, remote signals or barrier semaphores. Data moves between devices by JAX's collectives and lax.ppermute only.
A program may use at most 64 MiB of HBM per device.

v0:
```python
import jax
import jax.numpy as jnp
from jax import lax
from jax.sharding import PartitionSpec as P


def margin_terms(arrived, got_codes, risk_weights, correlation, funding_spread):
    path_rows = arrived.shape[0]
    cpty_count = funding_spread.shape[0]
    bucket_count = risk_weights.shape[0]
    is_filled = got_codes >= 0
    column_ids = jnp.arange(cpty_count * bucket_count, dtype=jnp.int32)
    hot_table = (got_codes[:, None] == column_ids[None, :]).astype(jnp.bfloat16)
    bucket_sums = jnp.dot(arrived, hot_table, preferred_element_type=jnp.float32)
    weighted = (
        bucket_sums.reshape(path_rows, cpty_count, bucket_count) * risk_weights[None, None, :]
    )
    rho_w = jnp.einsum("pcb,db->pcd", weighted, correlation, precision=lax.Precision.HIGHEST)
    margin_now = jnp.sqrt(jnp.sum(weighted * rho_w, axis=2) + 1e-06)
    sens_bar = (
        funding_spread[None, :, None] * risk_weights[None, None, :] * rho_w / margin_now[:, :, None]
    )
    flat_bar = sens_bar.reshape(path_rows, cpty_count * bucket_count)
    safe_codes = jnp.where(is_filled, got_codes, 0)
    slot_bar = jnp.take(flat_bar, safe_codes, axis=1) * is_filled[None, :].astype(jnp.float32)
    return (margin_now, slot_bar.astype(jnp.bfloat16))


def body(
    basis_values, coefficients, trade_cpty, trade_bucket, risk_weights, correlation, funding_spread
):
    owners = lax.axis_size("trade")
    per_device = coefficients.shape[0]
    capacity = max(2, 2 * per_device // owners)
    slot_total = owners * capacity
    cpty_count = funding_spread.shape[0]
    bucket_count = risk_weights.shape[0]
    path_rows = basis_values.shape[0]
    owner_of = trade_cpty // cpty_count
    trade_code = trade_cpty % cpty_count * bucket_count + trade_bucket
    position = jnp.arange(per_device, dtype=jnp.int32)
    same_owner = owner_of[:, None] == owner_of[None, :]
    earlier = position[None, :] < position[:, None]
    rank_in = jnp.sum((same_owner & earlier).astype(jnp.int32), axis=1)
    slot_index = owner_of * capacity + rank_in
    codes_out = jnp.full((slot_total,), -1, jnp.int32).at[slot_index].set(trade_code)
    got_codes = lax.all_to_all(codes_out, "trade", split_axis=0, concat_axis=0, tiled=True)
    delta_rows = lax.dot_general(
        basis_values, coefficients, (((1,), (1,)), ((), ())), preferred_element_type=jnp.float32
    ).astype(jnp.bfloat16)
    outgoing = jnp.zeros((path_rows, slot_total), jnp.bfloat16).at[:, slot_index].set(delta_rows)
    arrived = lax.all_to_all(outgoing, "trade", split_axis=1, concat_axis=1, tiled=True)
    margin_now, slot_bar = margin_terms(
        arrived, got_codes, risk_weights, correlation, funding_spread
    )
    returned = lax.all_to_all(slot_bar, "trade", split_axis=1, concat_axis=1, tiled=True)
    delta_bar = returned[:, slot_index]
    partial_adj = jnp.dot(delta_bar, coefficients, preferred_element_type=jnp.float32)
    basis_adjoint = lax.psum(partial_adj, "trade").astype(jnp.bfloat16)
    return (margin_now.T, basis_adjoint)


def solution(mesh):
    placed = (
        P(("date", "path"), None),
        P(("date", "trade"), None),
        P("trade"),
        P("trade"),
        P(),
        P(),
        P("trade"),
    )
    return jax.shard_map(
        body,
        mesh=mesh,
        in_specs=placed,
        out_specs=(P("trade", ("date", "path")), P(("date", "path"), None)),
        check_vma=False,
    )
```

profile of v0, /device:TPU:0, one launch (start us, length us, event | category | flops | bytes accessed | tf_op | source)
XLA Modules:
  0.0 130.3 jit_solution(14144373721821639996)
XLA Ops:
  0.6 0.8 fusion.14
  1.4 0.2 convert_reduce_fusion
  1.6 1.1 scatter_custom_fusion.1
  2.7 0.7 all_to_all.25
  3.4 7.3 %all-to-all-start.1 = ((s32[8,40,1]{1,2,0:T(1,128)}), s32[8,40,1]{1,2,0:T(1,128)S(1)}, u32[]{:S(2)}, u32[]{:S(2)}) async-start(s32[8,40,1]{1,2,0:T(1,128)} %all_to_all.25), calls=%async_computation.1 | async-start | bytes 8192 | tf_op jit(solution)/shard_map/all_to_all | solution.py:47
  10.7 1.2 fusion.7
  11.9 1.9 %scatter_custom_fusion = bf16[512,320]{0,1:T(8,128)(2,1)} fusion(s32[160]{0:T(256)S(1)} %compare_select_fusion.4, bf16[160,512]{1,0:T(8,128)(2,1)S(1)} %fusion.7, bf16[]{:T(256)} %constant.45.clone.1), kind=kCustom, calls=%fused_computation.18 | custom fusion | bytes 327682 | tf_op jit(solution)/shard_map/scatter | solution.py:51
  13.8 3.2 %all-to-all-done.1 = s32[8,40,1]{1,2,0:T(1,128)S(1)} async-done(((s32[8,40,1]{1,2,0:T(1,128)}), s32[8,40,1]{1,2,0:T(1,128)S(1)}, u32[]{:S(2)}, u32[]{:S(2)}) %all-to-all-start.1) | async-done | bytes 1312 | tf_op jit(solution)/shard_map/all_to_all | solution.py:47
  17.0 3.4 %all-to-all-start = ((bf16[512,8,40]{0,2,1:T(8,128)(2,1)}), bf16[512,8,40]{0,2,1:T(8,128)(2,1)S(1)}, u32[]{:S(2)}, u32[]{:S(2)}) async-start(bf16[512,8,40]{0,2,1:T(8,128)(2,1)} %bitcast.1), calls=%async_computation | async-start | bytes 655360 | tf_op jit(solution)/shard_map/all_to_all | solution.py:52
  20.5 0.7 broadcast_multiply_fusion
  21.2 0.5 broadcast.164
  21.7 0.7 reduce.7
  22.6 6.9 %all-to-all-done = bf16[512,8,40]{0,2,1:T(8,128)(2,1)S(1)} async-done(((bf16[512,8,40]{0,2,1:T(8,128)(2,1)}), bf16[512,8,40]{0,2,1:T(8,128)(2,1)S(1)}, u32[]{:S(2)}, u32[]{:S(2)}) %all-to-all-start) | async-done | bytes 327712 | tf_op jit(solution)/shard_map/all_to_all | solution.py:52
  29.6 1.4 %fusion.2 = f32[512,16,128]{0,2,1:T(8,128)S(1)} fusion(bf16[512,320,1]{0,1,2:T(8,128)(2,1)S(1)} %bitcast.29, s32[16,128]{1,0:T(8,128)S(1)} %multiply_add_fusion, s32[320]{0:T(512)S(1)} %eq.51), kind=kOutput, calls=%fused_computation.8 | convolution fusion | flops 671744000 | bytes 4531456 | tf_op jit(solution)/shard_map/dot_general | solution.py:14
  31.0 5.5 %multiply_reduce_fusion = (f32[512,16]{0,1:T(8,128)S(1)}, f32[512,16,128]{0,2,1:T(8,128)S(1)}) fusion(f32[512,16,128]{0,2,1:T(8,128)S(1)} %fusion.2, f32[128]{0:T(128)S(1)} %copy-done.3, f32[128,128]{1,0:T(8,128)S(1)} %copy-done.2), kind=kOutput, calls=%fused_computation.5 | convolution fusion | flops 1614798848 | bytes 8487424 | tf_op jit(solution)/shard_map/pcb,db->pcd/dot_general | solution.py:18
  36.4 0.6 add_sqrt_fusion
  37.1 2.4 %multiply_divide_fusion = f32[512,16,128]{0,2,1:T(8,128)} fusion(f32[512,16,128]{0,2,1:T(8,128)S(1)} %get-tuple-element.9, f32[512,16]{0,1:T(8,128)S(1)} %get-tuple-element.2, f32[16,128]{1,0:T(8,128)S(1)} %broadcast_multiply_fusion), kind=kLoop, calls=%fused_computation.4 | loop fusion | flops 2097152 | bytes 8429568 | tf_op jit(solution)/shard_map/div | solution.py:21
  39.5 4.3 %gather_fusion = f32[320,512]{1,0:T(8,128)S(1)} fusion(f32[512,2048]{0,1:T(8,128)} %bitcast.26, s32[1024]{0:T(1024)S(1)} %pad_clamp_fusion.1), kind=kCustom, calls=%fused_computation | custom fusion | bytes 1312000 | tf_op jit(solution)/shard_map/jit(_take)/gather | solution.py:25
  43.8 0.9 multiply_convert_fusion
  44.7 3.6 %all-to-all-start.2 = ((bf16[512,8,40]{0,2,1:T(8,128)(2,1)}), bf16[512,8,40]{0,2,1:T(8,128)(2,1)S(1)}, u32[]{:S(2)}, u32[]{:S(2)}) async-start(bf16[512,8,40]{0,2,1:T(8,128)(2,1)} %multiply_convert_fusion), calls=%async_computation.2 | async-start | bytes 655360 | tf_op jit(solution)/shard_map/all_to_all | solution.py:56
  48.3 9.6 %all-to-all-done.2 = bf16[512,8,40]{0,2,1:T(8,128)(2,1)S(1)} async-done(((bf16[512,8,40]{0,2,1:T(8,128)(2,1)}), bf16[512,8,40]{0,2,1:T(8,128)(2,1)S(1)}, u32[]{:S(2)}, u32[]{:S(2)}) %all-to-all-start.2) | async-done | bytes 327712 | tf_op jit(solution)/shard_map/all_to_all | solution.py:56
  57.9 0.9 gather_fusion.1
  58.8 0.3 fusion.18
  59.2 71.2 %all-reduce.1 = bf16[512,512]{1,0:T(8,128)(2,1)} all-reduce(f32[512,512]{1,0:T(8,128)S(1)} %fusion.18), channel_id=1, replica_groups=mesh['date'=2,'trade'=8,'path'=2] {'trade'}, use_global_device_ids=true, to_apply=%region_4.5 | all-reduce | flops 262144 | bytes 1572864 | tf_op jit(solution)/shard_map/psum | solution.py:59
  (16 shorter events, 0.2 us)
Async XLA Ops:
  0.6 10.0 %copy-start = (bf16[512,512]{1,0:T(8,128)(2,1)S(1)}, bf16[512,512]{1,0:T(8,128)(2,1)}, u32[]{:S(2)}) copy-start(bf16[512,512]{1,0:T(8,128)(2,1)} %param.7) | copy-start | bytes 1572868
  3.4 13.6 %all-to-all-start.1 = ((s32[8,40,1]{1,2,0:T(1,128)}), s32[8,40,1]{1,2,0:T(1,128)S(1)}, u32[]{:S(2)}, u32[]{:S(2)}) async-start(s32[8,40,1]{1,2,0:T(1,128)} %all_to_all.25), calls=%async_computation.1 | async-start | bytes 8192 | tf_op jit(solution)/shard_map/all_to_all | solution.py:47
  11.9 19.0 %copy-start.2 = (f32[128,128]{1,0:T(8,128)S(1)}, f32[128,128]{1,0:T(8,128)}, u32[]{:S(2)}) copy-start(f32[128,128]{1,0:T(8,128)} %param.12) | copy-start | bytes 196612
  11.9 19.0 %copy-start.3 = (f32[128]{0:T(128)S(1)}, f32[128]{0:T(128)}, u32[]{:S(2)}) copy-start(f32[128]{0:T(128)} %param.11) | copy-start | bytes 1540
  17.0 12.5 %all-to-all-start = ((bf16[512,8,40]{0,2,1:T(8,128)(2,1)}), bf16[512,8,40]{0,2,1:T(8,128)(2,1)S(1)}, u32[]{:S(2)}, u32[]{:S(2)}) async-start(bf16[512,8,40]{0,2,1:T(8,128)(2,1)} %bitcast.1), calls=%async_computation | async-start | bytes 655360 | tf_op jit(solution)/shard_map/all_to_all | solution.py:52
  39.5 19.3 %copy-start.1 = (bf16[160,512]{1,0:T(8,128)(2,1)S(1)}, bf16[160,512]{1,0:T(8,128)(2,1)}, u32[]{:S(2)}) copy-start(bf16[160,512]{1,0:T(8,128)(2,1)} %param.8) | copy-start | bytes 491524
  44.7 13.2 %all-to-all-start.2 = ((bf16[512,8,40]{0,2,1:T(8,128)(2,1)}), bf16[512,8,40]{0,2,1:T(8,128)(2,1)S(1)}, u32[]{:S(2)}, u32[]{:S(2)}) async-start(bf16[512,8,40]{0,2,1:T(8,128)(2,1)} %multiply_convert_fusion), calls=%async_computation.2 | async-start | bytes 655360 | tf_op jit(solution)/shard_map/all_to_all | solution.py:56
where the time goes:
time: 131 us; the launch traced here: 130 us
  blocking collectives  71.2 us (54%)
  waiting for transfers between devices  19.8 us (15%)
  starting transfers between devices  14.3 us (11%)
  local copies, waits for them, and re-layouts  9.56 us (7%)
  matrix products  8.42 us (6%)
  other arithmetic  6.37 us (5%)
    psum x1, blocking collectives, body(): basis_adjoint = lax.psum(partial_adj, 'trade').astype(jnp.bfloat16)  71.2 us
    all_to_all x1, waiting for transfers between devices, body(): lax.all_to_all(slot_bar, 'trade', split_axis=1, concat_axis=1, tiled=True)  9.6 us
    all_to_all x1, starting transfers between devices, body(): lax.all_to_all(codes_out, 'trade', split_axis=0, concat_axis=0, tiled=True)  7.25 us
    all_to_all x1, waiting for transfers between devices, body(): lax.all_to_all(outgoing, 'trade', split_axis=1, concat_axis=1, tiled=True)  6.93 us
    dot_general x1, matrix products, margin_terms(): jnp.einsum('pcb,db->pcd', weighted, correlation, precision=lax.Precision....  5.47 us
    gather x1, local copies, waits for them, and re-layouts, margin_terms(): jnp.take(flat_bar, safe_codes, axis=1)  4.27 us
    all_to_all x1, starting transfers between devices, body(): lax.all_to_all(slot_bar, 'trade', split_axis=1, concat_axis=1, tiled=True)  3.6 us
    all_to_all x1, starting transfers between devices, body(): lax.all_to_all(outgoing, 'trade', split_axis=1, concat_axis=1, tiled=True)  3.43 us
  transfers between devices with their start and end apart: 3, of which 3 were waited for; matrix products, arithmetic and copies ran while one was open for 4% of the time, Pallas kernels for 0%

commit v1 on v0

--- a/solution.py
+++ b/solution.py
@@ -1,7 +1,20 @@
+import functools
 import jax
 import jax.numpy as jnp
 from jax import lax
 from jax.sharding import PartitionSpec as P
+
+
+def _arrange_turns(raw, peer_axis):
+    small = jax.lax.axis_size(peer_axis)
+    piece_next = jnp.split(raw, small, axis=1)
+    step_out = jnp.stack(piece_next)
+    inter = jax.lax.all_to_all(step_out, peer_axis, 0, 0)
+    mat_out = jnp.concatenate(inter, axis=1)
+    return mat_out
+
+
+touch_plate = functools.partial(_arrange_turns, peer_axis="trade")
 
 
 def margin_terms(arrived, got_codes, risk_weights, correlation, funding_spread):
@@ -53,7 +66,7 @@
     margin_now, slot_bar = margin_terms(
         arrived, got_codes, risk_weights, correlation, funding_spread
     )
-    returned = lax.all_to_all(slot_bar, "trade", split_axis=1, concat_axis=1, tiled=True)
+    returned = touch_plate(slot_bar)
     delta_bar = returned[:, slot_index]
     partial_adj = jnp.dot(delta_bar, coefficients, preferred_element_type=jnp.float32)
     basis_adjoint = lax.psum(partial_adj, "trade").astype(jnp.bfloat16)

time: 131 us -> 135 us (1.031)
  local copies, waits for them, and re-layouts: 9.56 us -> 14.5 us
    unnamed x8 -> x15, local copies, waits for them, and re-layouts: 0.03 us -> 4.37 us
where the time goes in v1:
time: 135 us; the launch traced here: 134 us
  blocking collectives  71 us (53%)
  waiting for transfers between devices  19.8 us (15%)
  local copies, waits for them, and re-layouts  14.5 us (11%)
  starting transfers between devices  14.3 us (11%)
  matrix products  8.43 us (6%)
  other arithmetic  5.62 us (4%)
    psum x1, blocking collectives, body(): basis_adjoint = lax.psum(partial_adj, 'trade').astype(jnp.bfloat16)  71 us
    all_to_all x1, waiting for transfers between devices, _arrange_turns(): inter = jax.lax.all_to_all(step_out, peer_axis, 0, 0)  9.6 us
    all_to_all x1, starting transfers between devices, body(): lax.all_to_all(codes_out, 'trade', split_axis=0, concat_axis=0, tiled=True)  7.25 us
    all_to_all x1, waiting for transfers between devices, body(): lax.all_to_all(outgoing, 'trade', split_axis=1, concat_axis=1, tiled=True)  6.93 us
    dot_general x1, matrix products, margin_terms(): jnp.einsum('pcb,db->pcd', weighted, correlation, precision=lax.Precision....  5.48 us
    unnamed x15, local copies, waits for them, and re-layouts  4.37 us
    gather x1, local copies, waits for them, and re-layouts, margin_terms(): jnp.take(flat_bar, safe_codes, axis=1)  4.27 us
    all_to_all x1, starting transfers between devices, _arrange_turns(): inter = jax.lax.all_to_all(step_out, peer_axis, 0, 0)  3.59 us
  transfers between devices with their start and end apart: 3, of which 3 were waited for; matrix products, arithmetic and copies ran while one was open for 4% of the time, Pallas kernels for 0%

profile of v1, /device:TPU:0, one launch (start us, length us, event | category | flops | bytes accessed | tf_op | source)
XLA Modules:
  0.0 134.4 jit_solution(12626211795828763290)
XLA Ops:
  0.6 0.8 fusion.23
  1.6 1.1 scatter_custom_fusion.1
  2.7 0.7 all_to_all.22
  3.4 7.3 %all-to-all-start.1 = ((s32[8,40,1]{1,2,0:T(1,128)}), s32[8,40,1]{1,2,0:T(1,128)S(1)}, u32[]{:S(2)}, u32[]{:S(2)}) async-start(s32[8,40,1]{1,2,0:T(1,128)} %bitcast.4), calls=%async_computation.1 | async-start | bytes 8192 | tf_op jit(solution)/shard_map/all_to_all | solution.py:60
  10.6 1.2 fusion.7
  11.9 1.9 %scatter_custom_fusion = bf16[512,320]{0,1:T(8,128)(2,1)} fusion(s32[160]{0:T(256)S(1)} %compare_select_fusion.3, bf16[160,512]{1,0:T(8,128)(2,1)S(1)} %fusion.7, bf16[]{:T(256)} %constant.45.clone.1), kind=kCustom, calls=%fused_computation.19 | custom fusion | bytes 327682 | tf_op jit(solution)/shard_map/scatter | solution.py:64
  13.8 3.2 %all-to-all-done.1 = s32[8,40,1]{1,2,0:T(1,128)S(1)} async-done(((s32[8,40,1]{1,2,0:T(1,128)}), s32[8,40,1]{1,2,0:T(1,128)S(1)}, u32[]{:S(2)}, u32[]{:S(2)}) %all-to-all-start.1) | async-done | bytes 1312 | tf_op jit(solution)/shard_map/all_to_all | solution.py:60
  17.0 3.4 %all-to-all-start = ((bf16[512,8,40]{0,2,1:T(8,128)(2,1)}), bf16[512,8,40]{0,2,1:T(8,128)(2,1)S(1)}, u32[]{:S(2)}, u32[]{:S(2)}) async-start(bf16[512,8,40]{0,2,1:T(8,128)(2,1)} %bitcast.1), calls=%async_computation | async-start | bytes 655360 | tf_op jit(solution)/shard_map/all_to_all | solution.py:65
  20.5 0.7 broadcast_multiply_fusion
  21.7 0.7 reduce.7
  22.6 6.9 %all-to-all-done = bf16[512,8,40]{0,2,1:T(8,128)(2,1)S(1)} async-done(((bf16[512,8,40]{0,2,1:T(8,128)(2,1)}), bf16[512,8,40]{0,2,1:T(8,128)(2,1)S(1)}, u32[]{:S(2)}, u32[]{:S(2)}) %all-to-all-start) | async-done | bytes 327712 | tf_op jit(solution)/shard_map/all_to_all | solution.py:65
  29.5 1.4 %fusion.2 = f32[512,16,128]{0,2,1:T(8,128)S(1)} fusion(bf16[512,320,1]{0,1,2:T(8,128)(2,1)S(1)} %bitcast.61, s32[16,128]{1,0:T(8,128)S(1)} %multiply_add_fusion, s32[320]{0:T(512)S(1)} %eq.49), kind=kOutput, calls=%fused_computation.8 | convolution fusion | flops 671744000 | bytes 4531456 | tf_op jit(solution)/shard_map/dot_general | solution.py:27
  30.9 5.5 %multiply_reduce_fusion = (f32[512,16]{0,1:T(8,128)S(1)}, f32[512,16,128]{0,2,1:T(8,128)S(1)}) fusion(f32[512,16,128]{0,2,1:T(8,128)S(1)} %fusion.2, f32[128]{0:T(128)S(1)} %copy-done.3, f32[128,128]{1,0:T(8,128)S(1)} %copy-done.2), kind=kOutput, calls=%fused_computation.5 | convolution fusion | flops 1614798848 | bytes 8487424 | tf_op jit(solution)/shard_map/pcb,db->pcd/dot_general | solution.py:31
  36.4 0.6 add_sqrt_fusion
  37.1 2.4 %multiply_divide_fusion = f32[512,16,128]{0,2,1:T(8,128)} fusion(f32[512,16,128]{0,2,1:T(8,128)S(1)} %get-tuple-element.9, f32[512,16]{0,1:T(8,128)S(1)} %get-tuple-element.2, f32[16,128]{1,0:T(8,128)S(1)} %broadcast_multiply_fusion), kind=kLoop, calls=%fused_computation.4 | loop fusion | flops 2097152 | bytes 8429568 | tf_op jit(solution)/shard_map/div | solution.py:34
  39.5 4.3 %gather_fusion = f32[320,512]{1,0:T(8,128)S(1)} fusion(f32[512,2048]{0,1:T(8,128)} %bitcast.59, s32[1024]{0:T(1024)S(1)} %pad_clamp_fusion.1), kind=kCustom, calls=%fused_computation | custom fusion | bytes 1312000 | tf_op jit(solution)/shard_map/jit(_take)/gather | solution.py:38
  43.9 0.6 fusion.20
  44.5 0.6 fusion.19
  45.2 0.6 fusion.18
  45.8 0.6 fusion.17
  48.9 3.6 %all-to-all-start.2 = ((bf16[8,512,40]{1,2,0:T(8,128)(2,1)}), bf16[8,512,40]{1,2,0:T(8,128)(2,1)S(1)}, u32[]{:S(2)}, u32[]{:S(2)}) async-start(bf16[8,512,40]{1,2,0:T(8,128)(2,1)} %fusion.13), calls=%async_computation.2 | async-start | bytes 655360 | tf_op jit(solution)/shard_map/all_to_all | solution.py:12
  52.5 9.6 %all-to-all-done.2 = bf16[8,512,40]{1,2,0:T(8,128)(2,1)S(1)} async-done(((bf16[8,512,40]{1,2,0:T(8,128)(2,1)}), bf16[8,512,40]{1,2,0:T(8,128)(2,1)S(1)}, u32[]{:S(2)}, u32[]{:S(2)}) %all-to-all-start.2) | async-done | bytes 327712 | tf_op jit(solution)/shard_map/all_to_all | solution.py:12
  62.1 0.9 gather_fusion.1
  63.4 71.0 %all-reduce.1 = bf16[512,512]{1,0:T(8,128)(2,1)} all-reduce(f32[512,512]{1,0:T(8,128)S(1)} %fusion.27), channel_id=1, replica_groups=mesh['date'=2,'trade'=8,'path'=2] {'trade'}, use_global_device_ids=true, to_apply=%region_4.5 | all-reduce | flops 262144 | bytes 1572864 | tf_op jit(solution)/shard_map/psum | solution.py:72
  (24 shorter events, 3.9 us)
Async XLA Ops:
  0.6 10.0 %copy-start = (bf16[512,512]{1,0:T(8,128)(2,1)S(1)}, bf16[512,512]{1,0:T(8,128)(2,1)}, u32[]{:S(2)}) copy-start(bf16[512,512]{1,0:T(8,128)(2,1)} %param.7) | copy-start | bytes 1572868
  3.4 13.6 %all-to-all-start.1 = ((s32[8,40,1]{1,2,0:T(1,128)}), s32[8,40,1]{1,2,0:T(1,128)S(1)}, u32[]{:S(2)}, u32[]{:S(2)}) async-start(s32[8,40,1]{1,2,0:T(1,128)} %bitcast.4), calls=%async_computation.1 | async-start | bytes 8192 | tf_op jit(solution)/shard_map/all_to_all | solution.py:60
  11.9 19.0 %copy-start.2 = (f32[128,128]{1,0:T(8,128)S(1)}, f32[128,128]{1,0:T(8,128)}, u32[]{:S(2)}) copy-start(f32[128,128]{1,0:T(8,128)} %param.12) | copy-start | bytes 196612
  11.9 19.0 %copy-start.3 = (f32[128]{0:T(128)S(1)}, f32[128]{0:T(128)}, u32[]{:S(2)}) copy-start(f32[128]{0:T(128)} %param.11) | copy-start | bytes 1540
  17.0 12.5 %all-to-all-start = ((bf16[512,8,40]{0,2,1:T(8,128)(2,1)}), bf16[512,8,40]{0,2,1:T(8,128)(2,1)S(1)}, u32[]{:S(2)}, u32[]{:S(2)}) async-start(bf16[512,8,40]{0,2,1:T(8,128)(2,1)} %bitcast.1), calls=%async_computation | async-start | bytes 655360 | tf_op jit(solution)/shard_map/all_to_all | solution.py:65
  39.5 23.5 %copy-start.1 = (bf16[160,512]{1,0:T(8,128)(2,1)S(1)}, bf16[160,512]{1,0:T(8,128)(2,1)}, u32[]{:S(2)}) copy-start(bf16[160,512]{1,0:T(8,128)(2,1)} %param.8) | copy-start | bytes 491524
  48.9 13.2 %all-to-all-start.2 = ((bf16[8,512,40]{1,2,0:T(8,128)(2,1)}), bf16[8,512,40]{1,2,0:T(8,128)(2,1)S(1)}, u32[]{:S(2)}, u32[]{:S(2)}) async-start(bf16[8,512,40]{1,2,0:T(8,128)(2,1)} %fusion.13), calls=%async_computation.2 | async-start | bytes 655360 | tf_op jit(solution)/shard_map/all_to_all | solution.py:12
